TPU v7x, 32 devices: a whole 2x2x4 slice. The times are simulated.
32 devices in a mesh: dp: 2 (over x), ctx: 4 (over y, core), tp: 4 (over z).
Axes of the slice: x: 2, y: 2, z: 4, core: 2. Of those that a mesh axis runs over, the one named last changes fastest.
Arguments:
- tokens: bfloat16 [12, 1024, 768], P('dp', 'ctx'), may hold values from -6 to 6
- segments: int32 [12, 1024], P('dp', 'ctx'), may hold values from 0 to 15, never falling along the last dimension, each value on 1 to 512 neighbouring positions
- w_qkv: bfloat16 [768, 3, 768], P(('dp', 'ctx'), None, 'tp'), may hold values from -0.21875 to 0.21875
- q_bias: float32 [768], P('tp'), may hold values from -3 to 3
- v_bias: float32 [768], P('tp'), may hold values from -3 to 3
- w_out: bfloat16 [768, 768], P(('dp', 'ctx'), 'tp'), may hold values from -0.875 to 0.875
- out_bias: float32 [768], replicated, may hold values from -3 to 3
- gain_one: float32 [768], replicated, may hold values from 0.25 to 1.75
- shift_one: float32 [768], replicated, may hold values from -2 to 2
- w_in: bfloat16 [768, 3072], P(('dp', 'ctx'), 'tp'), may hold values from -0.21875 to 0.21875
- in_bias: float32 [3072], P('tp'), may hold values from -3 to 3
- w_back: bfloat16 [768, 3072], P(('dp', 'ctx'), 'tp'), may hold values from -0.15625 to 0.15625
- back_bias: float32 [768], replicated, may hold values from -3 to 3
- gain_two: float32 [768], replicated, may hold values from 0.25 to 1.75
- shift_two: float32 [768], replicated, may hold values from -2 to 2
- cotangent: bfloat16 [12, 1024, 768], P('dp', 'ctx'), may hold values from -6 to 6
Outputs:
- output: bfloat16 [12, 1024, 768], P('dp', 'ctx')
- d_tokens: float32 [12, 1024, 768], P('dp', 'ctx')
- d_w_qkv: float32 [768, 3, 768], P(('dp', 'ctx'), None, 'tp')
- d_q_bias: float32 [768], P('tp')
- d_v_bias: float32 [768], P('tp')
- d_w_out: float32 [768, 768], P(('dp', 'ctx'), 'tp')
- d_out_bias: float32 [768], replicated
- d_gain_one: float32 [768], replicated
- d_shift_one: float32 [768], replicated
- d_w_in: float32 [768, 3072], P(('dp', 'ctx'), 'tp')
- d_in_bias: float32 [3072], P('tp')
- d_w_back: float32 [768, 3072], P(('dp', 'ctx'), 'tp')
- d_back_bias: float32 [768], replicated
- d_gain_two: float32 [768], replicated
- d_shift_two: float32 [768], replicated
Inputs may be any that keep to these rules, and one draw needn't show every extreme that they name: `segments`: within one sequence segment numbers never fall; each of the 16 numbers covers 1 to 512 consecutive positions, one exactly 512.
All inputs are finite; a program needn't handle non-finite values.
Results may differ from a plain program's by a relative error of at most 0.013.
The roundings to bfloat16 on the way count: a program that leaves them out, or rounds other values in their place, can miss the bound.
Values may be sent and summed in bfloat16 or wider, within the bound.
A program may use at most 128 MiB of HBM per device.

v0:
```python
import math
import jax
import jax.numpy as jnp
from jax import lax
from jax.sharding import PartitionSpec as P

HEAD = 64


def norm_parts(value):
    mean = jnp.mean(value, -1, keepdims=True)
    centered = value - mean
    rstd = lax.rsqrt(jnp.mean(centered * centered, -1, keepdims=True) + 1e-12)
    return (centered * rstd, rstd)


def norm_back(grad, normal, rstd, gain):
    d_gain = jnp.sum(grad * normal, 0)
    d_shift = jnp.sum(grad, 0)
    scaled = grad * gain
    d_value = rstd * (
        scaled
        - jnp.mean(scaled, -1, keepdims=True)
        - normal * jnp.mean(scaled * normal, -1, keepdims=True)
    )
    return (d_value, d_gain, d_shift)


def gelu_slope(inner):
    return 0.5 * (1.0 + lax.erf(inner / math.sqrt(2.0))) + inner * jnp.exp(
        -0.5 * inner * inner
    ) / math.sqrt(2.0 * math.pi)


def masked_scores(q_heads, k_heads, seg_query, seg_key):
    raw = jnp.einsum("qhe,khe->hqk", q_heads, k_heads, preferred_element_type=jnp.float32)
    same = seg_query[:, None] == seg_key[None, :]
    return jnp.where(same[None], raw * (1.0 / math.sqrt(HEAD)), -1e30)


def per_device(
    tokens,
    segments,
    w_qkv,
    q_bias,
    v_bias,
    w_out,
    out_bias,
    gain_one,
    shift_one,
    w_in,
    in_bias,
    w_back,
    back_bias,
    gain_two,
    shift_two,
    cotangent,
):
    seqs, local_len, width = tokens.shape
    rows = seqs * local_len
    gathered = (
        lax.all_gather(w_qkv, ("dp", "ctx"), axis=0, tiled=True),
        lax.all_gather(w_out, ("dp", "ctx"), axis=0, tiled=True),
        lax.all_gather(w_in, ("dp", "ctx"), axis=0, tiled=True),
        lax.all_gather(w_back, ("dp", "ctx"), axis=0, tiled=True),
    )
    full_qkv, full_out, full_in, full_back = gathered
    col_width = full_out.shape[1]
    heads_here = col_width // HEAD
    x_rows = tokens.reshape(rows, width)
    grad_rows = cotangent.reshape(rows, width)
    projected = jnp.einsum("td,dcf->tcf", x_rows, full_qkv, preferred_element_type=jnp.float32)
    query = (projected[:, 0] + q_bias).astype(jnp.bfloat16).reshape(seqs, local_len, col_width)
    key = projected[:, 1].astype(jnp.bfloat16).reshape(seqs, local_len, col_width)
    value = (projected[:, 2] + v_bias).astype(jnp.bfloat16).reshape(seqs, local_len, col_width)
    key_full, value_full, seg_full = (
        lax.all_gather(key, "ctx", axis=1, tiled=True),
        lax.all_gather(value, "ctx", axis=1, tiled=True),
        lax.all_gather(segments, "ctx", axis=1, tiled=True),
    )
    full_len = key_full.shape[1]

    def attend(item):
        q_one, k_one, v_one, s_query, s_key = item
        q_heads = q_one.reshape(local_len, heads_here, HEAD)
        k_heads = k_one.reshape(full_len, heads_here, HEAD)
        v_heads = v_one.reshape(full_len, heads_here, HEAD)
        scores = masked_scores(q_heads, k_heads, s_query, s_key)
        peak = jnp.max(scores, -1, keepdims=True)
        expo = jnp.exp(scores - peak)
        total = jnp.sum(expo, -1, keepdims=True)
        probs_low = (expo / total).astype(jnp.bfloat16)
        context = jnp.einsum("hqk,khe->qhe", probs_low, v_heads, preferred_element_type=jnp.float32)
        lse = (peak + jnp.log(total))[..., 0]
        return (context.astype(jnp.bfloat16).reshape(local_len, col_width), lse)

    context, lse_kept = lax.map(attend, (query, key_full, value_full, segments, seg_full))
    context_rows = context.reshape(rows, col_width)
    attn_part = jnp.einsum("tf,df->td", context_rows, full_out, preferred_element_type=jnp.float32)
    attended = lax.psum(attn_part, "tp") + out_bias
    normal_one, rstd_one = norm_parts(x_rows.astype(jnp.float32) + attended)
    normed = normal_one * gain_one + shift_one
    normed_low = normed.astype(jnp.bfloat16)
    inner = jnp.dot(normed_low, full_in, preferred_element_type=jnp.float32) + in_bias
    active = jax.nn.gelu(inner, approximate=False).astype(jnp.bfloat16)
    ffn_part = jnp.einsum("tf,df->td", active, full_back, preferred_element_type=jnp.float32)
    second = normed + lax.psum(ffn_part, "tp") + back_bias
    normal_two, rstd_two = norm_parts(second)
    output = (normal_two * gain_two + shift_two).astype(jnp.bfloat16)
    d_second, d_gain_two, d_shift_two = norm_back(
        grad_rows.astype(jnp.float32), normal_two, rstd_two, gain_two
    )
    d_second_low = d_second.astype(jnp.bfloat16)
    d_back_bias = jnp.sum(d_second, 0)
    back_set = (
        lax.all_gather(w_qkv, ("dp", "ctx"), axis=0, tiled=True),
        lax.all_gather(w_out, ("dp", "ctx"), axis=0, tiled=True),
        lax.all_gather(w_in, ("dp", "ctx"), axis=0, tiled=True),
        lax.all_gather(w_back, ("dp", "ctx"), axis=0, tiled=True),
    )
    back_qkv, back_out, back_in, back_ffn = back_set
    d_w_back = jnp.einsum("td,tf->df", d_second_low, active, preferred_element_type=jnp.float32)
    d_active = jnp.dot(d_second_low, back_ffn, preferred_element_type=jnp.float32)
    d_inner = d_active * gelu_slope(inner)
    d_in_bias = jnp.sum(d_inner, 0)
    d_inner_low = d_inner.astype(jnp.bfloat16)
    d_w_in = jnp.einsum("td,tf->df", normed_low, d_inner_low, preferred_element_type=jnp.float32)
    hidden_part = jnp.einsum("tf,df->td", d_inner_low, back_in, preferred_element_type=jnp.float32)
    d_normed = lax.psum(hidden_part, "tp") + d_second
    d_first, d_gain_one, d_shift_one = norm_back(d_normed, normal_one, rstd_one, gain_one)
    d_first_low = d_first.astype(jnp.bfloat16)
    d_out_bias = jnp.sum(d_first, 0)
    d_w_out = jnp.einsum("td,tf->df", d_first_low, context_rows, preferred_element_type=jnp.float32)
    d_context = jnp.dot(d_first_low, back_out, preferred_element_type=jnp.float32).astype(
        jnp.bfloat16
    )
    d_context = d_context.reshape(seqs, local_len, col_width)

    def attend_back(item):
        q_one, k_one, v_one, s_query, s_key, lse, d_ctx = item
        q_heads = q_one.reshape(local_len, heads_here, HEAD)
        k_heads = k_one.reshape(full_len, heads_here, HEAD)
        v_heads = v_one.reshape(full_len, heads_here, HEAD)
        d_heads = d_ctx.reshape(local_len, heads_here, HEAD)
        scores = masked_scores(q_heads, k_heads, s_query, s_key)
        probs = jnp.exp(scores - lse[..., None])
        probs_low = probs.astype(jnp.bfloat16)
        d_probs = jnp.einsum("qhe,khe->hqk", d_heads, v_heads, preferred_element_type=jnp.float32)
        delta = jnp.sum(probs * d_probs, -1, keepdims=True)
        d_raw = (probs * (d_probs - delta) * (1.0 / math.sqrt(HEAD))).astype(jnp.bfloat16)
        d_query = jnp.einsum("hqk,khe->qhe", d_raw, k_heads, preferred_element_type=jnp.float32)
        d_key = jnp.einsum("hqk,qhe->khe", d_raw, q_heads, preferred_element_type=jnp.float32)
        d_value = jnp.einsum("hqk,qhe->khe", probs_low, d_heads, preferred_element_type=jnp.float32)
        return (
            d_query.reshape(local_len, col_width),
            d_key.reshape(full_len, col_width),
            d_value.reshape(full_len, col_width),
        )

    d_query, key_part, value_part = lax.map(
        attend_back, (query, key_full, value_full, segments, seg_full, lse_kept, d_context)
    )
    d_key, d_value = (
        lax.psum_scatter(key_part, "ctx", scatter_dimension=1, tiled=True),
        lax.psum_scatter(value_part, "ctx", scatter_dimension=1, tiled=True),
    )
    d_query = d_query.reshape(rows, col_width)
    d_value = d_value.reshape(rows, col_width)
    d_q_bias = jnp.sum(d_query, 0)
    d_v_bias = jnp.sum(d_value, 0)
    d_proj = jnp.stack([d_query, d_key.reshape(rows, col_width), d_value], 1).astype(jnp.bfloat16)
    d_w_qkv = jnp.einsum("td,tcf->dcf", x_rows, d_proj, preferred_element_type=jnp.float32)
    input_part = jnp.einsum("tcf,dcf->td", d_proj, back_qkv, preferred_element_type=jnp.float32)
    w_grads = (
        lax.psum_scatter(d_w_qkv, ("dp", "ctx"), scatter_dimension=0, tiled=True),
        lax.psum_scatter(d_w_out, ("dp", "ctx"), scatter_dimension=0, tiled=True),
        lax.psum_scatter(d_w_in, ("dp", "ctx"), scatter_dimension=0, tiled=True),
        lax.psum_scatter(d_w_back, ("dp", "ctx"), scatter_dimension=0, tiled=True),
    )
    d_tokens = lax.psum(input_part, "tp") + d_first
    small = lax.psum(
        (
            d_q_bias,
            d_v_bias,
            d_out_bias,
            d_gain_one,
            d_shift_one,
            d_in_bias,
            d_back_bias,
            d_gain_two,
            d_shift_two,
        ),
        ("dp", "ctx"),
    )
    return (
        output.reshape(seqs, local_len, width),
        d_tokens.reshape(seqs, local_len, width),
        w_grads[0],
        small[0],
        small[1],
        w_grads[1],
        small[2],
        small[3],
        small[4],
        w_grads[2],
        small[5],
        w_grads[3],
        small[6],
        small[7],
        small[8],
    )


def solution(mesh):
    return jax.shard_map(
        per_device,
        mesh=mesh,
        in_specs=(
            P("dp", "ctx", None),
            P("dp", "ctx"),
            P(("dp", "ctx"), None, "tp"),
            P("tp"),
            P("tp"),
            P(("dp", "ctx"), "tp"),
            P(),
            P(),
            P(),
            P(("dp", "ctx"), "tp"),
            P("tp"),
            P(("dp", "ctx"), "tp"),
            P(),
            P(),
            P(),
            P("dp", "ctx", None),
        ),
        out_specs=(
            P("dp", "ctx", None),
            P("dp", "ctx", None),
            P(("dp", "ctx"), None, "tp"),
            P("tp"),
            P("tp"),
            P(("dp", "ctx"), "tp"),
            P(),
            P(),
            P(),
            P(("dp", "ctx"), "tp"),
            P("tp"),
            P(("dp", "ctx"), "tp"),
            P(),
            P(),
            P(),
        ),
        check_vma=False,
    )
```

profile of v0, /device:TPU:0, one launch (start us, length us, event | category | flops | bytes accessed | tf_op | source)
XLA Modules:
  0.0 1147.8 jit_solution(3269655352616793134)
XLA Ops:
  9.1 14.6 %all_gather.25 = bf16[768,3,192]{2,1,0:T(4,128)(2,1)S(1)} all-gather(bf16[96,3,192]{2,1,0:T(4,128)(2,1)S(1)} %copy.55), channel_id=1, replica_groups=mesh['dp'=2,'ctx'=4,'tp'=4] {'dp','ctx'}, dimensions={0}, use_global_device_ids=true | all-gather | bytes 995328 | tf_op jit(solution)/shard_map/all_gather | solution.py:62
  38.0 5.8 all_gather.27
  43.9 11.6 %all_gather.29 = bf16[768,192]{1,0:T(8,128)(2,1)S(1)} all-gather(bf16[96,192]{1,0:T(8,128)(2,1)S(1)} %copy-done.17), channel_id=1, replica_groups=mesh['dp'=2,'ctx'=4,'tp'=4] {'dp','ctx'}, dimensions={0}, use_global_device_ids=true | all-gather | bytes 331776 | tf_op jit(solution)/shard_map/all_gather | solution.py:63
  55.5 7.2 all-gather.7.cloned.1.call-done
  65.8 28.0 %all-gather.5.cloned.1.call-done = bf16[6,1024,192]{1,0,2:T(8,128)(2,1)} async-done(((bf16[6,256,192]{1,0,2:T(8,128)(2,1)}), bf16[6,1024,192]{1,0,2:T(8,128)(2,1)}) %all-gather.5.cloned.1.call-update) | async-done | bytes 2359312 | tf_op jit(solution)/shard_map/all_gather | solution.py:78
  93.8 4.6 copy.57
  98.4 40.9 %while.26 = (s32[]{:T(128)}, bf16[6,256,192]{1,2,0:T(8,128)(2,1)}, f32[6,3,256]{2,1,0:T(4,128)}, bf16[6,1024,192]{1,2,0:T(8,128)(2,1)}, s32[6,256]{1,0:T(8,128)}...) while((s32[]{:T(128)}, bf16[6,256,192]{1,2,0:T(8,128)(2,1)}, ...), condition=%wide.region_3.4_spmd, body=%wide.region_0.3_spmd.sunk | while | flops 211074304 | bytes 13475965 | solution.py:97
  146.1 170.7 %all-reduce.6.cloned.1.call-done = f32[1536,768]{1,0:T(8,128)} async-done(((f32[1536,768]{1,0:T(8,128)}), f32[1536,768]{1,0:T(8,128)}) %all-reduce.6.cloned.1.call-update) | async-done | bytes 4718608 | tf_op jit(solution)/shard_map/psum | solution.py:100
  323.6 14.6 %fusion.26 = (bf16[1536,768]{1,0:T(8,128)(2,1)S(1)}, f32[1536,768]{1,0:T(8,128)}) fusion(f32[768]{0:T(1024)S(1)} %copy-done.37, bf16[768,768]{1,0:T(8,128)(2,1)} %all-gather.9.cloned.1.call-done, f32[1536,768]{1,0:T(8,128)} %copy-done, f32[768]{0:T(1024)S(1)} %copy-done.31, f32[768]{0:T(1024)S(1)} %copy-done.19, f32[1536]{0:T(1024)S(1)} %add_rsqrt_fusion.1, ...), kind=kOutput, calls=%fused_computation.47 | convolution fusion | flops 1895694336 | bytes 12997632 | tf_op jit(solution)/shard_map/dot_general | solution.py:104
  339.6 5.5 fusion.71
  348.4 167.8 %all-reduce.8.cloned.1.call-done = f32[1536,768]{1,0:T(8,128)} async-done(((f32[1536,768]{1,0:T(8,128)}), f32[1536,768]{1,0:T(8,128)}) %all-reduce.8.cloned.1.call-update) | async-done | bytes 4718608 | tf_op jit(solution)/shard_map/psum | solution.py:107
  516.2 4.7 fusion.60
  538.1 170.8 %all-reduce.10.cloned.1.call-done = f32[1536,768]{1,0:T(8,128)} async-done(((f32[1536,768]{1,0:T(8,128)}), f32[1536,768]{1,0:T(8,128)}) %all-reduce.10.cloned.1.call-update) | async-done | bytes 4718608 | tf_op jit(solution)/shard_map/psum | solution.py:129
  708.9 7.1 multiply_reduce_fusion.1
  723.7 123.8 %while.27 = (s32[]{:T(128)}, f32[6,256,192]{1,2,0:T(8,128)}, f32[6,1024,192]{1,2,0:T(8,128)}, f32[6,1024,192]{1,2,0:T(8,128)}, bf16[6,1024,192]{1,2,0:T(8,128)(2...) while((s32[]{:T(128)}, f32[6,256,192]{1,2,0:T(8,128)}, ...), condition=%wide.region_17.18_spmd, body=%wide.region_15.17_spmd.sunk | while | flops 514592256 | bytes 45572424 | solution.py:160
  797.4 4.5 fusion.140
  850.8 43.7 %reduce-scatter.9.cloned.1.call-done = f32[6,256,192]{1,2,0:T(8,128)} async-done(((f32[6,1024,192]{1,2,0:T(8,128)}), f32[6,256,192]{1,2,0:T(8,128)}) %reduce-scatter.9.cloned.1.call-update) | async-done | bytes 1179664 | tf_op jit(solution)/shard_map/reduce_scatter | solution.py:164
  896.9 48.2 %reduce-scatter.11.cloned.1.call-done = f32[6,256,192]{1,2,0:T(8,128)} async-done(((f32[6,1024,192]{1,2,0:T(8,128)}), f32[6,256,192]{1,2,0:T(8,128)}) %reduce-scatter.11.cloned.1.call-update) | async-done | bytes 1179664 | tf_op jit(solution)/shard_map/reduce_scatter | solution.py:165
  955.5 5.7 convolution_bitcast_fusion
  961.3 7.0 fusion.54
  968.4 7.0 fusion.50
  979.9 25.9 %all-reduce = (f32[192]{0:T(256)}, f32[192]{0:T(256)}, f32[768]{0:T(1024)}, f32[768]{0:T(1024)}, f32[768]{0:T(1024)}, /*index=5*/f32[768]{0:T(1024)}, f32[768]{0:T(1024)}, f32[768]{0:T(1024)}, f32[768]{0:T(1024)}) all-reduce(f32[192]{0:T(256)S(1)} %get-tuple-element.291, ...), channel_id=1, replica_groups=mesh['dp'=2,'ctx'=4,'tp'=4] {'dp','ctx'}, use_global_device_ids=true, to_apply=%region_23.24 | all-reduce | flops 5760 | bytes 46080 | tf_op jit(solution)/shard_map/psum | solution.py:181
  1007.8 125.5 %all-reduce.12.cloned.1.call-done = f32[1536,768]{1,0:T(8,128)} async-done(((f32[1536,768]{1,0:T(8,128)}), f32[1536,768]{1,0:T(8,128)}) %all-reduce.12.cloned.1.call-update) | async-done | bytes 4718608 | tf_op jit(solution)/shard_map/psum | solution.py:180
  1133.3 6.6 add.172
  (383 shorter events, 243.3 us)
Async XLA Ops:
  8.0 54.6 %all-gather.7.cloned.1.call-start = ((), (), s32[]{:S(2)}) async-start(), calls=%async_computation.7 | async-start | bytes 3932160 | tf_op jit(solution)/shard_map/all_gather | solution.py:77
  24.6 5.4 copy-start.15
  30.1 6.0 copy-start.33
  31.6 62.2 %all-gather.5.cloned.1.call-start = ((), (), s32[]{:S(2)}) async-start(), calls=%async_computation.6 | async-start | bytes 3932160 | tf_op jit(solution)/shard_map/all_gather | solution.py:78
  36.0 7.8 copy-start.17
  37.2 279.6 %all-reduce.6.cloned.1.call-start = ((), (), s32[]{:S(2)}) async-start(), calls=%async_computation.8 | async-start | bytes 9437184 | tf_op jit(solution)/shard_map/psum | solution.py:100
  141.7 175.2 %copy-start.27 = (f32[768]{0:T(1024)S(1)}, f32[768]{0:T(1024)}, u32[]{:S(2)}) copy-start(f32[768]{0:T(1024)} %param.26) | copy-start | bytes 9220
  144.7 178.8 %all-gather.9.cloned.1.call-start = ((), (), s32[]{:S(2)}) async-start(), calls=%async_computation.9 | async-start | bytes 1327104 | tf_op jit(solution)/shard_map/all_gather | solution.py:64
  145.3 192.9 %all-gather.11.cloned.1.call-start = ((), (), s32[]{:S(2)}) async-start(), calls=%async_computation.10 | async-start | bytes 1327104 | tf_op jit(solution)/shard_map/all_gather | solution.py:65
  145.9 370.3 %all-reduce.8.cloned.1.call-start = ((), (), s32[]{:S(2)}) async-start(), calls=%async_computation.11 | async-start | bytes 9437184 | tf_op jit(solution)/shard_map/psum | solution.py:107
  345.1 171.1 %copy-start.30 = (f32[768]{0:T(1024)S(1)}, f32[768]{0:T(1024)}, u32[]{:S(2)}) copy-start(f32[768]{0:T(1024)} %param.32) | copy-start | bytes 9220
  345.1 363.8 %all-reduce.10.cloned.1.call-start = ((), (), s32[]{:S(2)}) async-start(), calls=%async_computation.12 | async-start | bytes 9437184 | tf_op jit(solution)/shard_map/psum | solution.py:129
  521.6 6.5 slice-start
  528.1 5.5 copy-start.35
  537.8 356.7 %reduce-scatter.9.cloned.1.call-start = ((), (), s32[]{:S(2)}) async-start(), calls=%async_computation.13 | async-start | bytes 5898240 | tf_op jit(solution)/shard_map/reduce_scatter | solution.py:164
  847.5 97.6 %reduce-scatter.11.cloned.1.call-start = ((), (), s32[]{:S(2)}) async-start(), calls=%async_computation.14 | async-start | bytes 5898240 | tf_op jit(solution)/shard_map/reduce_scatter | solution.py:165
  848.3 157.6 %reduce-scatter.19.cloned.1.call-start = ((), (), s32[]{:S(2)}) async-start(), calls=%async_computation.19 | async-start | bytes 2211840
  955.2 178.1 %all-reduce.12.cloned.1.call-start = ((), (), s32[]{:S(2)}) async-start(), calls=%async_computation.15 | async-start | bytes 9437184 | tf_op jit(solution)/shard_map/psum | solution.py:180
  961.2 7.1 copy-start.20
  961.2 7.1 copy-start.32
  961.2 178.6 %reduce-scatter.17.cloned.1.call-start = ((), (), s32[]{:S(2)}) async-start(), calls=%async_computation.18 | async-start | bytes 2654208 | tf_op jit(solution)/shard_map/reduce_scatter | solution.py:178
  968.3 7.3 copy-start.8
  968.3 171.6 %reduce-scatter.15.cloned.1.call-start = ((), (), s32[]{:S(2)}) async-start(), calls=%async_computation.17 | async-start | bytes 2654208 | tf_op jit(solution)/shard_map/reduce_scatter | solution.py:177
  975.5 164.4 %reduce-scatter.13.cloned.1.call-start = ((), (), s32[]{:S(2)}) async-start(), calls=%async_computation.16 | async-start | bytes 884736 | tf_op jit(solution)/shard_map/reduce_scatter | solution.py:176
  (62 other events, 210.0 us)
Sparse Core Ops, SparseCore 0:
  31.7 30.8 all-gather.6
  64.8 28.9 all-gather.4
  144.8 171.9 all-reduce.5
  345.2 170.9 all-reduce.7
  537.9 170.9 all-reduce.9
  847.7 46.8 reduce-scatter.8
  897.2 47.8 reduce-scatter.10
  961.3 171.9 all-reduce.11
Sparse Core Ops, SparseCore 1:
  147.1 23.9 all-gather.8
  172.8 23.9 all-gather.10
  955.2 40.2 reduce-scatter.18
  999.8 42.4 reduce-scatter.16
  1046.2 42.3 reduce-scatter.14
  1092.6 34.9 reduce-scatter.12
where the time goes:
time: 1160 us; the launch traced here: 1150 us
  waiting for transfers between devices  764 us (66%)
  matrix products  159 us (14%)
  local copies, waits for them, and re-layouts  96.2 us (8%)
  blocking collectives  58 us (5%)
  other arithmetic  52.4 us (5%)
  between operations  16.7 us (1%)
    psum x1, waiting for transfers between devices, per_device(): d_normed = lax.psum(hidden_part, 'tp') + d_second  171 us
    psum x1, waiting for transfers between devices, per_device(): attended = lax.psum(attn_part, 'tp') + out_bias  171 us
    psum x1, waiting for transfers between devices, per_device(): second = normed + lax.psum(ffn_part, 'tp') + back_bias  168 us
    psum x1, waiting for transfers between devices, per_device(): d_tokens = lax.psum(input_part, 'tp') + d_first  125 us
    reduce_scatter x1, waiting for transfers between devices, per_device(): lax.psum_scatter(value_part, 'ctx', scatter_dimension=1, tiled=True)  48.2 us
    reduce_scatter x1, waiting for transfers between devices, per_device(): lax.psum_scatter(key_part, 'ctx', scatter_dimension=1, tiled=True)  43.7 us
    dynamic_slice x60, local copies, waits for them, and re-layouts, per_device(): lax.map(attend, (query, key_full, value_full, segments, seg_full))  36.6 us
    all_gather x1, waiting for transfers between devices, per_device(): lax.all_gather(value, 'ctx', axis=1, tiled=True)  28 us
  transfers between devices with their start and end apart: 14, of which 8 were waited for; matrix products, arithmetic and copies ran while one was open for 6% of the time, Pallas kernels for 0%

commit v1 on v0

--- a/solution.py
+++ b/solution.py
@@ -5,6 +5,12 @@
 from jax.sharding import PartitionSpec as P
 
 HEAD = 64
+
+
+def summed_here(block, mesh_axis):
+    terms = lax.all_gather(block, mesh_axis, axis=0, tiled=False)
+    total = terms.sum(axis=0)
+    return total
 
 
 def norm_parts(value):
@@ -104,7 +110,7 @@
     inner = jnp.dot(normed_low, full_in, preferred_element_type=jnp.float32) + in_bias
     active = jax.nn.gelu(inner, approximate=False).astype(jnp.bfloat16)
     ffn_part = jnp.einsum("tf,df->td", active, full_back, preferred_element_type=jnp.float32)
-    second = normed + lax.psum(ffn_part, "tp") + back_bias
+    second = normed + summed_here(ffn_part, "tp") + back_bias
     normal_two, rstd_two = norm_parts(second)
     output = (normal_two * gain_two + shift_two).astype(jnp.bfloat16)
     d_second, d_gain_two, d_shift_two = norm_back(

time: 1160 us -> 1310 us (1.13)
  waiting for transfers between devices: 764 us -> 918 us
    all_gather x0 -> x1, waiting for transfers between devices: none -> 319 us  [summed_here(): terms = lax.all_gather(block, mesh_axis, axis=0, tiled=False)]
    psum x1 -> x0, waiting for transfers between devices: 168 us -> none  [per_device(): second = normed + lax.psum(ffn_part, 'tp') + back_bias]
    all_gather x1, waiting for transfers between devices: 7.2 us -> 26.5 us  [per_device(): lax.all_gather(key, 'ctx', axis=1, tiled=True)]
    all_gather x1, waiting for transfers between devices: 28 us -> 10.5 us  [per_device(): lax.all_gather(value, 'ctx', axis=1, tiled=True)]
  transfers between devices with their start and end apart: 14 -> 14, of which waited for: 8 -> 8; matrix products, arithmetic and copies ran while one was open for 6% -> 5% of each run, Pallas kernels for 0% -> 0%
where the time goes in v1:
time: 1310 us; the launch traced here: 1300 us
  waiting for transfers between devices  918 us (70%)
  matrix products  157 us (12%)
  local copies, waits for them, and re-layouts  94.8 us (7%)
  blocking collectives  55.9 us (4%)
  other arithmetic  55.7 us (4%)
  between operations  16.7 us (1%)
    all_gather x1, waiting for transfers between devices, summed_here(): terms = lax.all_gather(block, mesh_axis, axis=0, tiled=False)  319 us
    psum x1, waiting for transfers between devices, per_device(): attended = lax.psum(attn_part, 'tp') + out_bias  171 us
    psum x1, waiting for transfers between devices, per_device(): d_normed = lax.psum(hidden_part, 'tp') + d_second  171 us
    psum x1, waiting for transfers between devices, per_device(): d_tokens = lax.psum(input_part, 'tp') + d_first  127 us
    reduce_scatter x1, waiting for transfers between devices, per_device(): lax.psum_scatter(value_part, 'ctx', scatter_dimension=1, tiled=True)  48.2 us
    reduce_scatter x1, waiting for transfers between devices, per_device(): lax.psum_scatter(key_part, 'ctx', scatter_dimension=1, tiled=True)  43.8 us
    dynamic_slice x60, local copies, waits for them, and re-layouts, per_device(): lax.map(attend, (query, key_full, value_full, segments, seg_full))  36.5 us
    dot_general x6, matrix products, attend_back(): jnp.einsum('hqk,qhe->khe', d_raw, q_heads, preferred_element_type=jnp.flo...  27.3 us
  transfers between devices with their start and end apart: 14, of which 8 were waited for; matrix products, arithmetic and copies ran while one was open for 5% of the time, Pallas kernels for 0%

profile of v1, /device:TPU:0, one launch (start us, length us, event | category | flops | bytes accessed | tf_op | source)
XLA Modules:
  0.0 1300.4 jit_solution(9154560759312034379)
XLA Ops:
  9.1 14.6 %all_gather.31 = bf16[768,3,192]{2,1,0:T(4,128)(2,1)S(1)} all-gather(bf16[96,3,192]{2,1,0:T(4,128)(2,1)S(1)} %copy.55), channel_id=1, replica_groups=mesh['dp'=2,'ctx'=4,'tp'=4] {'dp','ctx'}, dimensions={0}, use_global_device_ids=true | all-gather | bytes 995328 | tf_op jit(solution)/shard_map/all_gather | solution.py:68
  37.7 5.2 all_gather.33
  42.9 10.7 all_gather.35
  53.6 10.5 all-gather.7.cloned.1.call-done
  64.1 4.6 copy.57
  68.7 26.5 %all-gather.9.cloned.1.call-done = bf16[6,1024,192]{1,0,2:T(8,128)(2,1)} async-done(((bf16[6,256,192]{1,0,2:T(8,128)(2,1)}), bf16[6,1024,192]{1,0,2:T(8,128)(2,1)}) %all-gather.9.cloned.1.call-update) | async-done | bytes 2359312 | tf_op jit(solution)/shard_map/all_gather | solution.py:83
  99.8 31.2 %while.26 = (s32[]{:T(128)}, bf16[6,256,192]{1,2,0:T(8,128)(2,1)S(1)}, f32[6,3,256]{2,1,0:T(4,128)S(1)}, bf16[6,1024,192]{1,2,0:T(8,128)(2,1)}, s32[6,256]{1,0:T...) while((s32[]{:T(128)}, ...), condition=%wide.region_3.4_spmd, body=%wide.region_0.3_spmd.sunk | while | flops 211074304 | bytes 13478005 | solution.py:103
  136.3 170.7 %all-reduce.5.cloned.1.call-done = f32[1536,768]{1,0:T(8,128)} async-done(((f32[1536,768]{1,0:T(8,128)}), f32[1536,768]{1,0:T(8,128)}) %all-reduce.5.cloned.1.call-update) | async-done | bytes 4718608 | tf_op jit(solution)/shard_map/psum | solution.py:106
  313.0 14.6 %fusion.26 = (bf16[1536,768]{1,0:T(8,128)(2,1)S(1)}, f32[1536,768]{1,0:T(8,128)}) fusion(f32[768]{0:T(1024)S(1)} %copy-done.24, bf16[768,768]{1,0:T(8,128)(2,1)} %all-gather.11.cloned.1.call-done, f32[1536,768]{1,0:T(8,128)} %copy-done, f32[768]{0:T(1024)S(1)} %copy-done.19, f32[768]{0:T(1024)S(1)} %copy-done.15, f32[1536]{0:T(1024)S(1)} %add_rsqrt_fusion.1, ...), kind=kOutput, calls=%fused_computation.47 | convolution fusion | flops 1895694336 | bytes 12997632 | tf_op jit(solution)/shard_map/dot_general | solution.py:110
  329.2 5.5 fusion.71
  337.5 318.9 %all-gather.15.cloned.1.call-done = f32[6144,768]{1,0:T(8,128)} async-done(((f32[1536,768]{1,0:T(8,128)}), f32[6144,768]{1,0:T(8,128)}) %all-gather.15.cloned.1.call-update) | async-done | bytes 18874384 | tf_op jit(solution)/shard_map/all_gather | solution.py:11
  656.5 10.5 reduce_sum.182
  667.0 4.7 fusion.60
  687.2 170.6 %all-reduce.7.cloned.1.call-done = f32[1536,768]{1,0:T(8,128)} async-done(((f32[1536,768]{1,0:T(8,128)}), f32[1536,768]{1,0:T(8,128)}) %all-reduce.7.cloned.1.call-update) | async-done | bytes 4718608 | tf_op jit(solution)/shard_map/psum | solution.py:135
  857.8 6.5 multiply_reduce_fusion.1
  872.3 127.8 %while.27 = (s32[]{:T(128)}, f32[6,256,192]{1,2,0:T(8,128)}, f32[6,1024,192]{1,2,0:T(8,128)}, f32[6,1024,192]{1,2,0:T(8,128)}, bf16[6,1024,192]{1,2,0:T(8,128)(2...) while((s32[]{:T(128)}, f32[6,256,192]{1,2,0:T(8,128)}, ...), condition=%wide.region_17.18_spmd, body=%wide.region_15.17_spmd.sunk | while | flops 514592256 | bytes 32990380 | solution.py:166
  1003.4 43.8 %reduce-scatter.9.cloned.1.call-done = f32[6,256,192]{1,2,0:T(8,128)} async-done(((f32[6,1024,192]{1,2,0:T(8,128)}), f32[6,256,192]{1,2,0:T(8,128)}) %reduce-scatter.9.cloned.1.call-update) | async-done | bytes 1179664 | tf_op jit(solution)/shard_map/reduce_scatter | solution.py:170
  1049.5 48.2 %reduce-scatter.11.cloned.1.call-done = f32[6,256,192]{1,2,0:T(8,128)} async-done(((f32[6,1024,192]{1,2,0:T(8,128)}), f32[6,256,192]{1,2,0:T(8,128)}) %reduce-scatter.11.cloned.1.call-update) | async-done | bytes 1179664 | tf_op jit(solution)/shard_map/reduce_scatter | solution.py:171
  1108.1 5.6 convolution_bitcast_fusion
  1113.9 7.6 fusion.50
  1121.6 5.8 fusion.54
  1131.9 25.4 %all-reduce = (f32[192]{0:T(256)}, f32[192]{0:T(256)}, f32[768]{0:T(1024)}, f32[768]{0:T(1024)}, f32[768]{0:T(1024)}, /*index=5*/f32[768]{0:T(1024)}, f32[768]{0:T(1024)}, f32[768]{0:T(1024)}, f32[768]{0:T(1024)}) all-reduce(f32[192]{0:T(256)S(1)} %get-tuple-element.291, ...), channel_id=1, replica_groups=mesh['dp'=2,'ctx'=4,'tp'=4] {'dp','ctx'}, use_global_device_ids=true, to_apply=%region_23.24 | all-reduce | flops 5760 | bytes 46080 | tf_op jit(solution)/shard_map/psum | solution.py:187
  1159.3 126.7 %all-reduce.9.cloned.1.call-done = f32[1536,768]{1,0:T(8,128)} async-done(((f32[1536,768]{1,0:T(8,128)}), f32[1536,768]{1,0:T(8,128)}) %all-reduce.9.cloned.1.call-update) | async-done | bytes 4718608 | tf_op jit(solution)/shard_map/psum | solution.py:186
  1285.9 6.6 add.170
  (310 shorter events, 239.1 us)
Async XLA Ops:
  8.0 56.1 %all-gather.7.cloned.1.call-start = ((), (), s32[]{:S(2)}) async-start(), calls=%async_computation.6 | async-start | bytes 3932160 | tf_op jit(solution)/shard_map/all_gather | solution.py:84
  33.2 9.8 copy-start.12
  33.2 62.0 %all-gather.9.cloned.1.call-start = ((), (), s32[]{:S(2)}) async-start(), calls=%async_computation.7 | async-start | bytes 3932160 | tf_op jit(solution)/shard_map/all_gather | solution.py:83
  36.1 270.9 %all-reduce.5.cloned.1.call-start = ((), (), s32[]{:S(2)}) async-start(), calls=%async_computation.8 | async-start | bytes 9437184 | tf_op jit(solution)/shard_map/psum | solution.py:106
  131.9 175.2 %copy-start.8 = (bf16[6,256,768]{2,1,0:T(8,128)(2,1)S(1)}, bf16[6,256,768]{2,1,0:T(8,128)(2,1)}, u32[]{:S(2)}) copy-start(bf16[6,256,768]{2,1,0:T(8,128)(2,1)} %param.20) | copy-start | bytes 7077892
  131.9 175.2 %copy-start.16 = (f32[768]{0:T(1024)S(1)}, f32[768]{0:T(1024)}, u32[]{:S(2)}) copy-start(f32[768]{0:T(1024)} %param.26) | copy-start | bytes 9220
  134.9 178.0 %all-gather.11.cloned.1.call-start = ((), (), s32[]{:S(2)}) async-start(), calls=%async_computation.9 | async-start | bytes 1327104 | tf_op jit(solution)/shard_map/all_gather | solution.py:70
  135.5 192.1 %all-gather.13.cloned.1.call-start = ((), (), s32[]{:S(2)}) async-start(), calls=%async_computation.10 | async-start | bytes 1327104 | tf_op jit(solution)/shard_map/all_gather | solution.py:71
  136.1 520.4 %all-gather.15.cloned.1.call-start = ((), (), s32[]{:S(2)}) async-start(), calls=%async_computation.18 | async-start | bytes 23592960 | tf_op jit(solution)/shard_map/all_gather | solution.py:11
  334.7 523.1 %all-reduce.7.cloned.1.call-start = ((), (), s32[]{:S(2)}) async-start(), calls=%async_computation.11 | async-start | bytes 9437184 | tf_op jit(solution)/shard_map/psum | solution.py:135
  656.5 10.5 copy-start.18
  686.9 360.3 %reduce-scatter.9.cloned.1.call-start = ((), (), s32[]{:S(2)}) async-start(), calls=%async_computation.12 | async-start | bytes 5898240 | tf_op jit(solution)/shard_map/reduce_scatter | solution.py:170
  916.1 5.6 copy-start.4
  937.4 5.6 copy-start.4
  958.7 5.6 copy-start.4
  980.1 5.6 copy-start.4
  1000.2 97.5 %reduce-scatter.11.cloned.1.call-start = ((), (), s32[]{:S(2)}) async-start(), calls=%async_computation.13 | async-start | bytes 5898240 | tf_op jit(solution)/shard_map/reduce_scatter | solution.py:171
  1000.9 156.3 %reduce-scatter.19.cloned.1.call-start = ((), (), s32[]{:S(2)}) async-start(), calls=%async_computation.19 | async-start | bytes 2211840
  1107.8 178.1 %all-reduce.9.cloned.1.call-start = ((), (), s32[]{:S(2)}) async-start(), calls=%async_computation.14 | async-start | bytes 9437184 | tf_op jit(solution)/shard_map/psum | solution.py:186
  1113.8 7.7 copy-start.26
  1113.8 178.7 %reduce-scatter.15.cloned.1.call-start = ((), (), s32[]{:S(2)}) async-start(), calls=%async_computation.16 | async-start | bytes 2654208 | tf_op jit(solution)/shard_map/reduce_scatter | solution.py:183
  1121.5 6.0 copy-start.6
  1121.5 171.0 %reduce-scatter.17.cloned.1.call-start = ((), (), s32[]{:S(2)}) async-start(), calls=%async_computation.17 | async-start | bytes 2654208 | tf_op jit(solution)/shard_map/reduce_scatter | solution.py:184
  1127.4 165.1 %reduce-scatter.13.cloned.1.call-start = ((), (), s32[]{:S(2)}) async-start(), calls=%async_computation.15 | async-start | bytes 884736 | tf_op jit(solution)/shard_map/reduce_scatter | solution.py:182
  (25 other events, 75.8 us)
Sparse Core Ops, SparseCore 0:
  33.3 30.8 all-gather.6
  66.2 28.9 all-gather.8
  135.0 171.9 all-reduce.4
  334.9 321.5 all-gather.14
  687.0 170.7 all-reduce.6
  1000.3 46.8 reduce-scatter.8
  1049.9 47.7 reduce-scatter.10
  1113.9 171.9 all-reduce.8
Sparse Core Ops, SparseCore 1:
  137.3 23.9 all-gather.10
  163.0 23.9 all-gather.12
  1107.9 40.3 reduce-scatter.18
  1152.5 42.3 reduce-scatter.14
  1198.8 42.3 reduce-scatter.16
  1245.3 34.9 reduce-scatter.12
